TPU v7x, 32 devices: a whole 2x2x4 slice. The times are simulated.
32 devices in a mesh: hist: 4 (over y, x), row: 4 (over z), cur: 2 (over core).
Axes of the slice: x: 2, y: 2, z: 4, core: 2. Of those that a mesh axis runs over, the one named last changes fastest.
Arguments:
- incident: bfloat16 [4, 32, 256, 64], P(None, ('hist', 'row', 'cur')), may hold values from -6 to 6
- past: bfloat16 [32, 8, 256, 64], P(('hist', 'row', 'cur')), may hold values from -6 to 6
- hist_tiles: bfloat16 [32, 64, 256, 256], P(('hist', 'row', 'cur')), may hold values from -0.046875 to 0.046875
- tile_rows: int32 [32, 64], P(('hist', 'row', 'cur')), may hold values from 0 to 3
- tile_cols: int32 [32, 64], P(('hist', 'row', 'cur')), may hold values from 0 to 7
- tile_lags: int32 [32, 64], P(('hist', 'row', 'cur')), may hold values from 4 to 8
- tile_scales: float32 [32, 64], P(('hist', 'row', 'cur')), may hold values from 0.5 to 2
- near_tiles: bfloat16 [32, 3, 5, 256, 256], P(('hist', 'row', 'cur')), may hold values from -0.09375 to 0.09375
- inverses: bfloat16 [32, 256, 256], P(('hist', 'row', 'cur')), may hold values from -0.21875 to 0.21875
Outputs:
- densities: bfloat16 [4, 32, 256, 64], P(None, ('hist', 'row', 'cur'))
All inputs are finite; a program needn't handle non-finite values.
Results may differ from a plain program's by a relative error of at most 0.02.
Values may be sent and summed in bfloat16 or wider, within the bound.
No kernel may reach another device: no remote copies, remote signals or barrier semaphores. Data moves between devices by JAX's collectives and lax.ppermute only.
A program may use at most 128 MiB of HBM per device.

v0:
```python
import jax
import jax.numpy as jnp
from jax import lax
from jax.sharding import PartitionSpec as P


def shifted(block, axis, distance):
    devices = range(lax.axis_size(axis))
    route = [(i - distance, i) for i in devices if i - distance in devices]
    return lax.ppermute(block, axis, route)


def window_cycle(window):
    pieces = []
    for amount in (2, 1, 0, -1, -2):
        if amount == 0:
            pieces.append(window)
        else:
            pieces.append(shifted(window, ("hist", "row", "cur"), amount))
    return jnp.stack(pieces)


def on_device(
    incident, past, hist_tiles, tile_rows, tile_cols, tile_lags, tile_scales, near_tiles, inverses
):
    step_count = incident.shape[0]
    kept = past.shape[1]
    group_past = lax.all_gather(past, ("row", "cur"), axis=0, tiled=True)
    when = jnp.arange(step_count, dtype=jnp.int32)[:, None] - tile_lags[0][None, :] + kept
    picked = group_past[tile_cols[0][None, :], when]
    terms = jnp.einsum("kij,skjr->skir", hist_tiles[0], picked, preferred_element_type=jnp.float32)
    terms = terms * tile_scales[0][None, :, None, None]
    terms_high = terms.astype(jnp.bfloat16)
    terms_low = (terms - terms_high.astype(jnp.float32)).astype(jnp.bfloat16)
    targets = tile_rows[0]
    owners = jnp.arange(lax.axis_size("hist"), dtype=jnp.int32)
    onehot = (targets[None, :] == owners[:, None]).astype(jnp.bfloat16)
    upper = jnp.einsum("gk,skir->gsir", onehot, terms_high, preferred_element_type=jnp.float32)
    lower = jnp.einsum("gk,skir->gsir", onehot, terms_low, preferred_element_type=jnp.float32)
    history = lax.psum_scatter(
        (upper + lower).astype(jnp.bfloat16), "hist", scatter_dimension=0, tiled=True
    ).astype(jnp.float32)
    window = past[0, kept - 3 :]
    made = []
    for step in range(step_count):
        cycle = window_cycle(window)
        arranged = jnp.swapaxes(cycle[:, ::-1], 0, 1)
        near = jnp.einsum(
            "loij,lojr->ir", near_tiles[0], arranged, preferred_element_type=jnp.float32
        )
        rhs = (incident[step, 0].astype(jnp.float32) - history[0, step] - near).astype(jnp.bfloat16)
        fresh = jnp.dot(inverses[0], rhs, preferred_element_type=jnp.float32).astype(jnp.bfloat16)
        made.append(fresh)
        window = jnp.concatenate([window[1:], fresh[None]], axis=0)
    return jnp.stack(made)[:, None]


def solution(mesh):
    placed = (
        P(None, ("hist", "row", "cur"), None, None),
        P(("hist", "row", "cur"), None, None, None),
        P(("hist", "row", "cur"), None, None, None),
        P(("hist", "row", "cur"), None),
        P(("hist", "row", "cur"), None),
        P(("hist", "row", "cur"), None),
        P(("hist", "row", "cur"), None),
        P(("hist", "row", "cur"), None, None, None, None),
        P(("hist", "row", "cur"), None, None),
    )
    return jax.shard_map(
        on_device,
        mesh=mesh,
        in_specs=placed,
        out_specs=P(None, ("hist", "row", "cur"), None, None),
        check_vma=False,
    )
```

profile of v0, /device:TPU:26, one launch (start us, length us, event | category | flops | bytes accessed | tf_op | source)
XLA Modules:
  0.0 180.7 jit_solution(2788014744332403338)
XLA Ops:
  8.2 3.0 %collective-permute-start = (bf16[3,256,64]{1,2,0:T(8,128)(2,1)S(1)}, bf16[3,256,64]{1,2,0:T(8,128)(2,1)S(1)}, u32[]{:S(2)}, u32[]{:S(2)}) collective-permute-start(bf16[3,256,64]{1,2,0:T(8,128)(2,1)S(1)} %slice_bitcast_fusion), channel_id=1, source_target_pairs={{0,2},{1,3},{2,4},{3,5},{4,6},{5,7},{6,8},{7,9},{8,10},{9,11},{10,... | collective-permute-start | bytes 294920 | tf_op jit(solution)/shard_map/ppermute | solution.py:10
  11.3 1.9 %collective-permute-start.1 = (bf16[3,256,64]{1,2,0:T(8,128)(2,1)S(1)}, bf16[3,256,64]{1,2,0:T(8,128)(2,1)S(1)}, u32[]{:S(2)}, u32[]{:S(2)}) collective-permute-start(bf16[3,256,64]{1,2,0:T(8,128)(2,1)S(1)} %slice_bitcast_fusion), channel_id=1, source_target_pairs={{0,1},{1,2},{2,3},{3,4},{4,5},{5,6},{6,7},{7,8},{8,9},{9,10},{10,1... | collective-permute-start | bytes 294920 | tf_op jit(solution)/shard_map/ppermute | solution.py:10
  13.2 3.6 %collective-permute-start.2 = (bf16[3,256,64]{1,2,0:T(8,128)(2,1)S(1)}, bf16[3,256,64]{1,2,0:T(8,128)(2,1)S(1)}, u32[]{:S(2)}, u32[]{:S(2)}) collective-permute-start(bf16[3,256,64]{1,2,0:T(8,128)(2,1)S(1)} %slice_bitcast_fusion), channel_id=1, source_target_pairs={{1,0},{2,1},{3,2},{4,3},{5,4},{6,5},{7,6},{8,7},{9,8},{10,9},{11,1... | collective-permute-start | bytes 294920 | tf_op jit(solution)/shard_map/ppermute | solution.py:10
  16.8 2.8 %collective-permute-start.3 = (bf16[3,256,64]{1,2,0:T(8,128)(2,1)S(1)}, bf16[3,256,64]{1,2,0:T(8,128)(2,1)S(1)}, u32[]{:S(2)}, u32[]{:S(2)}) collective-permute-start(bf16[3,256,64]{1,2,0:T(8,128)(2,1)S(1)} %slice_bitcast_fusion), channel_id=1, source_target_pairs={{2,0},{3,1},{4,2},{5,3},{6,4},{7,5},{8,6},{9,7},{10,8},{11,9},{12,... | collective-permute-start | bytes 294920 | tf_op jit(solution)/shard_map/ppermute | solution.py:10
  21.9 18.8 %all-gather.2.cloned.1.call-done = bf16[8,8,256,64]{2,3,1,0:T(8,128)(2,1)} async-done(((bf16[1,8,256,64]{2,3,1,0:T(8,128)(2,1)}), bf16[8,8,256,64]{2,3,1,0:T(8,128)(2,1)}) %all-gather.2.cloned.1.call-update) | async-done | bytes 2097168 | tf_op jit(solution)/shard_map/all_gather | solution.py:28
  40.7 11.7 %gather_fusion = bf16[256,256,64]{1,2,0:T(8,128)(2,1)} fusion(bf16[8,8,256,64]{2,3,1,0:T(8,128)(2,1)} %all-gather.2.cloned.1.call-done, s32[256]{0:T(256)S(1)} %reshape.64), kind=kCustom, calls=%fused_computation | custom fusion | bytes 16779264 | tf_op jit(solution)/shard_map/gather | solution.py:30
  52.4 15.9 %fusion = (bf16[4,64,256,64]{2,3,0,1:T(8,128)(2,1)}, f32[64,4,64,256]{3,2,1,0:T(8,128)}) fusion(f32[64]{0:T(128)S(1)} %bitcast.219, bf16[1,64,256,256]{3,2,1,0:T(8,128)(2,1)} %param.11, bf16[4,64,256,64]{2,3,1,0:T(8,128)(2,1)} %bitcast.218), kind=kOutput, calls=%fused_computation.3 | convolution fusion | flops 2168455168 | bytes 41943296 | tf_op jit(solution)/shard_map/kij,skjr->skir/dot_general | solution.py:31
  68.3 8.1 %bitcast_convert_fusion = bf16[4,64,256,64]{2,3,0,1:T(8,128)(2,1)S(1)} fusion(f32[64,4,64,256]{3,2,1,0:T(8,128)} %get-tuple-element.6, f32[64]{0:T(128)S(1)} %bitcast.220), kind=kLoop, calls=%fused_computation.2 | loop fusion | flops 8388608 | bytes 25166080 | tf_op jit(solution)/shard_map/convert_element_type | solution.py:33
  76.5 4.6 %fusion.3 = f32[4,4,256,64]{2,0,3,1:T(4,128)S(1)} fusion(bf16[4,64,256,64]{2,3,0,1:T(8,128)(2,1)S(1)} %copy-done.1, s32[64]{0:T(128)S(1)} %bitcast.221), kind=kOutput, calls=%fused_computation.6 | convolution fusion | flops 33554688 | bytes 9437440 | tf_op jit(solution)/shard_map/gk,skir->gsir/dot_general | solution.py:39
  81.1 4.7 %fusion.19 = bf16[4,4,256,64]{2,0,3,1:T(4,128)(2,1)S(1)} fusion(f32[4,4,256,64]{2,0,3,1:T(4,128)S(1)} %fusion.3, bf16[4,64,256,64]{2,3,0,1:T(8,128)(2,1)S(1)} %bitcast_convert_fusion, s32[64]{0:T(128)S(1)} %bitcast.222), kind=kOutput, calls=%fused_computation.20 | convolution fusion | flops 34078976 | bytes 9961728 | tf_op jit(solution)/shard_map/gk,skir->gsir/dot_general | solution.py:38
  87.8 25.1 %reduce-scatter.4.cloned.1.call-done = bf16[1,4,256,64]{2,3,1,0:T(8,128)(2,1)} async-done(((bf16[4,4,256,64]{2,3,1,0:T(8,128)(2,1)}), bf16[1,4,256,64]{2,3,1,0:T(8,128)(2,1)}) %reduce-scatter.4.cloned.1.call-update) | async-done | bytes 131088
  114.7 3.3 %collective-permute-start.4 = (bf16[3,256,64]{1,2,0:T(8,128)(2,1)S(1)}, bf16[3,256,64]{1,2,0:T(8,128)(2,1)S(1)}, u32[]{:S(2)}, u32[]{:S(2)}) collective-permute-start(bf16[3,256,64]{1,2,0:T(8,128)(2,1)S(1)} %pad_maximum_fusion), channel_id=1, source_target_pairs={{0,2},{1,3},{2,4},{3,5},{4,6},{5,7},{6,8},{7,9},{8,10},{9,11},{10,... | collective-permute-start | bytes 294920 | tf_op jit(solution)/shard_map/ppermute | solution.py:10
  118.0 1.9 %collective-permute-start.5 = (bf16[3,256,64]{1,2,0:T(8,128)(2,1)S(1)}, bf16[3,256,64]{1,2,0:T(8,128)(2,1)S(1)}, u32[]{:S(2)}, u32[]{:S(2)}) collective-permute-start(bf16[3,256,64]{1,2,0:T(8,128)(2,1)S(1)} %pad_maximum_fusion), channel_id=1, source_target_pairs={{0,1},{1,2},{2,3},{3,4},{4,5},{5,6},{6,7},{7,8},{8,9},{9,10},{10,1... | collective-permute-start | bytes 294920 | tf_op jit(solution)/shard_map/ppermute | solution.py:10
  120.0 3.6 %collective-permute-start.6 = (bf16[3,256,64]{1,2,0:T(8,128)(2,1)S(1)}, bf16[3,256,64]{1,2,0:T(8,128)(2,1)S(1)}, u32[]{:S(2)}, u32[]{:S(2)}) collective-permute-start(bf16[3,256,64]{1,2,0:T(8,128)(2,1)S(1)} %pad_maximum_fusion), channel_id=1, source_target_pairs={{1,0},{2,1},{3,2},{4,3},{5,4},{6,5},{7,6},{8,7},{9,8},{10,9},{11,1... | collective-permute-start | bytes 294920 | tf_op jit(solution)/shard_map/ppermute | solution.py:10
  123.6 2.5 %collective-permute-start.7 = (bf16[3,256,64]{1,2,0:T(8,128)(2,1)S(1)}, bf16[3,256,64]{1,2,0:T(8,128)(2,1)S(1)}, u32[]{:S(2)}, u32[]{:S(2)}) collective-permute-start(bf16[3,256,64]{1,2,0:T(8,128)(2,1)S(1)} %pad_maximum_fusion), channel_id=1, source_target_pairs={{2,0},{3,1},{4,2},{5,3},{6,4},{7,5},{8,6},{9,7},{10,8},{11,9},{12,... | collective-permute-start | bytes 294920 | tf_op jit(solution)/shard_map/ppermute | solution.py:10
  126.3 7.4 %collective-permute-done.7 = bf16[3,256,64]{1,2,0:T(8,128)(2,1)S(1)} collective-permute-done((bf16[3,256,64]{1,2,0:T(8,128)(2,1)S(1)}, bf16[3,256,64]{1,2,0:T(8,128)(2,1)S(1)}, u32[]{:S(2)}, u32[]{:S(2)}) %collective-permute-start.7) | collective-permute-done | bytes 98336 | tf_op jit(solution)/shard_map/ppermute | solution.py:10
  134.7 3.4 %collective-permute-start.8 = (bf16[3,256,64]{1,2,0:T(8,128)(2,1)S(1)}, bf16[3,256,64]{1,2,0:T(8,128)(2,1)S(1)}, u32[]{:S(2)}, u32[]{:S(2)}) collective-permute-start(bf16[3,256,64]{1,2,0:T(8,128)(2,1)S(1)} %pad_maximum_fusion.1), channel_id=1, source_target_pairs={{0,2},{1,3},{2,4},{3,5},{4,6},{5,7},{6,8},{7,9},{8,10},{9,11},{10,... | collective-permute-start | bytes 294920 | tf_op jit(solution)/shard_map/ppermute | solution.py:10
  138.0 1.9 %collective-permute-start.9 = (bf16[3,256,64]{1,2,0:T(8,128)(2,1)S(1)}, bf16[3,256,64]{1,2,0:T(8,128)(2,1)S(1)}, u32[]{:S(2)}, u32[]{:S(2)}) collective-permute-start(bf16[3,256,64]{1,2,0:T(8,128)(2,1)S(1)} %pad_maximum_fusion.1), channel_id=1, source_target_pairs={{0,1},{1,2},{2,3},{3,4},{4,5},{5,6},{6,7},{7,8},{8,9},{9,10},{10,1... | collective-permute-start | bytes 294920 | tf_op jit(solution)/shard_map/ppermute | solution.py:10
  140.0 3.6 %collective-permute-start.10 = (bf16[3,256,64]{1,2,0:T(8,128)(2,1)S(1)}, bf16[3,256,64]{1,2,0:T(8,128)(2,1)S(1)}, u32[]{:S(2)}, u32[]{:S(2)}) collective-permute-start(bf16[3,256,64]{1,2,0:T(8,128)(2,1)S(1)} %pad_maximum_fusion.1), channel_id=1, source_target_pairs={{1,0},{2,1},{3,2},{4,3},{5,4},{6,5},{7,6},{8,7},{9,8},{10,9},{11,1... | collective-permute-start | bytes 294920 | tf_op jit(solution)/shard_map/ppermute | solution.py:10
  143.6 2.5 %collective-permute-start.11 = (bf16[3,256,64]{1,2,0:T(8,128)(2,1)S(1)}, bf16[3,256,64]{1,2,0:T(8,128)(2,1)S(1)}, u32[]{:S(2)}, u32[]{:S(2)}) collective-permute-start(bf16[3,256,64]{1,2,0:T(8,128)(2,1)S(1)} %pad_maximum_fusion.1), channel_id=1, source_target_pairs={{2,0},{3,1},{4,2},{5,3},{6,4},{7,5},{8,6},{9,7},{10,8},{11,9},{12,... | collective-permute-start | bytes 294920 | tf_op jit(solution)/shard_map/ppermute | solution.py:10
  146.2 7.5 %collective-permute-done.11 = bf16[3,256,64]{1,2,0:T(8,128)(2,1)S(1)} collective-permute-done((bf16[3,256,64]{1,2,0:T(8,128)(2,1)S(1)}, bf16[3,256,64]{1,2,0:T(8,128)(2,1)S(1)}, u32[]{:S(2)}, u32[]{:S(2)}) %collective-permute-start.11) | collective-permute-done | bytes 98336 | tf_op jit(solution)/shard_map/ppermute | solution.py:10
  158.5 3.6 %collective-permute-start.14 = (bf16[3,256,64]{1,2,0:T(8,128)(2,1)S(1)}, bf16[3,256,64]{1,2,0:T(8,128)(2,1)S(1)}, u32[]{:S(2)}, u32[]{:S(2)}) collective-permute-start(bf16[3,256,64]{1,2,0:T(8,128)(2,1)S(1)} %pad_maximum_fusion.2), channel_id=1, source_target_pairs={{1,0},{2,1},{3,2},{4,3},{5,4},{6,5},{7,6},{8,7},{9,8},{10,9},{11,1... | collective-permute-start | bytes 294920 | tf_op jit(solution)/shard_map/ppermute | solution.py:10
  162.2 3.9 %collective-permute-start.15 = (bf16[3,256,64]{1,2,0:T(8,128)(2,1)S(1)}, bf16[3,256,64]{1,2,0:T(8,128)(2,1)S(1)}, u32[]{:S(2)}, u32[]{:S(2)}) collective-permute-start(bf16[3,256,64]{1,2,0:T(8,128)(2,1)S(1)} %pad_maximum_fusion.2), channel_id=1, source_target_pairs={{2,0},{3,1},{4,2},{5,3},{6,4},{7,5},{8,6},{9,7},{10,8},{11,9},{12,... | collective-permute-start | bytes 294920 | tf_op jit(solution)/shard_map/ppermute | solution.py:10
  166.2 6.1 %collective-permute-done.15 = bf16[3,256,64]{1,2,0:T(8,128)(2,1)S(1)} collective-permute-done((bf16[3,256,64]{1,2,0:T(8,128)(2,1)S(1)}, bf16[3,256,64]{1,2,0:T(8,128)(2,1)S(1)}, u32[]{:S(2)}, u32[]{:S(2)}) %collective-permute-start.15) | collective-permute-done | bytes 98336 | tf_op jit(solution)/shard_map/ppermute | solution.py:10
  (72 shorter events, 15.1 us)
Async XLA Ops:
  6.5 107.3 %copy-start = (bf16[1,3,5,256,256]{4,3,2,1,0:T(8,128)(2,1)S(1)}, bf16[1,3,5,256,256]{4,3,2,1,0:T(8,128)(2,1)}, u32[]{:S(2)}) copy-start(bf16[1,3,5,256,256]{4,3,2,1,0:T(8,128)(2,1)} %param.16) | copy-start | bytes 5898244
  6.5 34.2 %all-gather.2.cloned.1.call-start = ((), (), s32[]{:S(2)}) async-start(), calls=%async_computation.1 | async-start | bytes 2359296 | tf_op jit(solution)/shard_map/all_gather | solution.py:28
  7.3 105.6 %reduce-scatter.4.cloned.1.call-start = ((), (), s32[]{:S(2)}) async-start(), calls=%async_computation.2 | async-start | bytes 655360
  8.2 78.5 %collective-permute-start = (bf16[3,256,64]{1,2,0:T(8,128)(2,1)S(1)}, bf16[3,256,64]{1,2,0:T(8,128)(2,1)S(1)}, u32[]{:S(2)}, u32[]{:S(2)}) collective-permute-start(bf16[3,256,64]{1,2,0:T(8,128)(2,1)S(1)} %slice_bitcast_fusion), channel_id=1, source_target_pairs={{0,2},{1,3},{2,4},{3,5},{4,6},{5,7},{6,8},{7,9},{8,10},{9,11},{10,... | collective-permute-start | bytes 294920 | tf_op jit(solution)/shard_map/ppermute | solution.py:10
  11.3 75.5 %collective-permute-start.1 = (bf16[3,256,64]{1,2,0:T(8,128)(2,1)S(1)}, bf16[3,256,64]{1,2,0:T(8,128)(2,1)S(1)}, u32[]{:S(2)}, u32[]{:S(2)}) collective-permute-start(bf16[3,256,64]{1,2,0:T(8,128)(2,1)S(1)} %slice_bitcast_fusion), channel_id=1, source_target_pairs={{0,1},{1,2},{2,3},{3,4},{4,5},{5,6},{6,7},{7,8},{8,9},{9,10},{10,1... | collective-permute-start | bytes 294920 | tf_op jit(solution)/shard_map/ppermute | solution.py:10
  13.2 74.5 %collective-permute-start.2 = (bf16[3,256,64]{1,2,0:T(8,128)(2,1)S(1)}, bf16[3,256,64]{1,2,0:T(8,128)(2,1)S(1)}, u32[]{:S(2)}, u32[]{:S(2)}) collective-permute-start(bf16[3,256,64]{1,2,0:T(8,128)(2,1)S(1)} %slice_bitcast_fusion), channel_id=1, source_target_pairs={{1,0},{2,1},{3,2},{4,3},{5,4},{6,5},{7,6},{8,7},{9,8},{10,9},{11,1... | collective-permute-start | bytes 294920 | tf_op jit(solution)/shard_map/ppermute | solution.py:10
  16.8 70.8 %collective-permute-start.3 = (bf16[3,256,64]{1,2,0:T(8,128)(2,1)S(1)}, bf16[3,256,64]{1,2,0:T(8,128)(2,1)S(1)}, u32[]{:S(2)}, u32[]{:S(2)}) collective-permute-start(bf16[3,256,64]{1,2,0:T(8,128)(2,1)S(1)} %slice_bitcast_fusion), channel_id=1, source_target_pairs={{2,0},{3,1},{4,2},{5,3},{6,4},{7,5},{8,6},{9,7},{10,8},{11,9},{12,... | collective-permute-start | bytes 294920 | tf_op jit(solution)/shard_map/ppermute | solution.py:10
  21.9 30.5 %copy-start.4 = (f32[1,64]{1,0:T(1,128)S(1)}, f32[1,64]{1,0:T(1,128)}, u32[]{:S(2)}) copy-start(f32[1,64]{1,0:T(1,128)} %param.15) | copy-start | bytes 772
  68.3 8.2 %copy-start.1 = (bf16[4,64,256,64]{2,3,0,1:T(8,128)(2,1)S(1)}, bf16[4,64,256,64]{2,3,0,1:T(8,128)(2,1)}, u32[]{:S(2)}) copy-start(bf16[4,64,256,64]{2,3,0,1:T(8,128)(2,1)} %get-tuple-element.5) | copy-start | bytes 25165828
  68.3 8.2 %copy-start.5 = (s32[1,64]{1,0:T(1,128)S(1)}, s32[1,64]{1,0:T(1,128)}, u32[]{:S(2)}) copy-start(s32[1,64]{1,0:T(1,128)} %param.12) | copy-start | bytes 772
  81.1 32.7 %copy-start.2 = (bf16[1,256,256]{2,1,0:T(8,128)(2,1)S(1)}, bf16[1,256,256]{2,1,0:T(8,128)(2,1)}, u32[]{:S(2)}) copy-start(bf16[1,256,256]{2,1,0:T(8,128)(2,1)} %param.17) | copy-start | bytes 393220
  81.1 32.7 %copy-start.3 = (bf16[4,1,256,64]{2,3,1,0:T(8,128)(2,1)S(1)}, bf16[4,1,256,64]{2,3,1,0:T(8,128)(2,1)}, u32[]{:S(2)}) copy-start(bf16[4,1,256,64]{2,3,1,0:T(8,128)(2,1)} %param.9) | copy-start | bytes 393220
  114.7 11.5 %collective-permute-start.4 = (bf16[3,256,64]{1,2,0:T(8,128)(2,1)S(1)}, bf16[3,256,64]{1,2,0:T(8,128)(2,1)S(1)}, u32[]{:S(2)}, u32[]{:S(2)}) collective-permute-start(bf16[3,256,64]{1,2,0:T(8,128)(2,1)S(1)} %pad_maximum_fusion), channel_id=1, source_target_pairs={{0,2},{1,3},{2,4},{3,5},{4,6},{5,7},{6,8},{7,9},{8,10},{9,11},{10,... | collective-permute-start | bytes 294920 | tf_op jit(solution)/shard_map/ppermute | solution.py:10
  118.0 8.2 %collective-permute-start.5 = (bf16[3,256,64]{1,2,0:T(8,128)(2,1)S(1)}, bf16[3,256,64]{1,2,0:T(8,128)(2,1)S(1)}, u32[]{:S(2)}, u32[]{:S(2)}) collective-permute-start(bf16[3,256,64]{1,2,0:T(8,128)(2,1)S(1)} %pad_maximum_fusion), channel_id=1, source_target_pairs={{0,1},{1,2},{2,3},{3,4},{4,5},{5,6},{6,7},{7,8},{8,9},{9,10},{10,1... | collective-permute-start | bytes 294920 | tf_op jit(solution)/shard_map/ppermute | solution.py:10
  120.0 6.3 %collective-permute-start.6 = (bf16[3,256,64]{1,2,0:T(8,128)(2,1)S(1)}, bf16[3,256,64]{1,2,0:T(8,128)(2,1)S(1)}, u32[]{:S(2)}, u32[]{:S(2)}) collective-permute-start(bf16[3,256,64]{1,2,0:T(8,128)(2,1)S(1)} %pad_maximum_fusion), channel_id=1, source_target_pairs={{1,0},{2,1},{3,2},{4,3},{5,4},{6,5},{7,6},{8,7},{9,8},{10,9},{11,1... | collective-permute-start | bytes 294920 | tf_op jit(solution)/shard_map/ppermute | solution.py:10
  123.6 10.1 %collective-permute-start.7 = (bf16[3,256,64]{1,2,0:T(8,128)(2,1)S(1)}, bf16[3,256,64]{1,2,0:T(8,128)(2,1)S(1)}, u32[]{:S(2)}, u32[]{:S(2)}) collective-permute-start(bf16[3,256,64]{1,2,0:T(8,128)(2,1)S(1)} %pad_maximum_fusion), channel_id=1, source_target_pairs={{2,0},{3,1},{4,2},{5,3},{6,4},{7,5},{8,6},{9,7},{10,8},{11,9},{12,... | collective-permute-start | bytes 294920 | tf_op jit(solution)/shard_map/ppermute | solution.py:10
  134.7 11.5 %collective-permute-start.8 = (bf16[3,256,64]{1,2,0:T(8,128)(2,1)S(1)}, bf16[3,256,64]{1,2,0:T(8,128)(2,1)S(1)}, u32[]{:S(2)}, u32[]{:S(2)}) collective-permute-start(bf16[3,256,64]{1,2,0:T(8,128)(2,1)S(1)} %pad_maximum_fusion.1), channel_id=1, source_target_pairs={{0,2},{1,3},{2,4},{3,5},{4,6},{5,7},{6,8},{7,9},{8,10},{9,11},{10,... | collective-permute-start | bytes 294920 | tf_op jit(solution)/shard_map/ppermute | solution.py:10
  138.0 8.1 %collective-permute-start.9 = (bf16[3,256,64]{1,2,0:T(8,128)(2,1)S(1)}, bf16[3,256,64]{1,2,0:T(8,128)(2,1)S(1)}, u32[]{:S(2)}, u32[]{:S(2)}) collective-permute-start(bf16[3,256,64]{1,2,0:T(8,128)(2,1)S(1)} %pad_maximum_fusion.1), channel_id=1, source_target_pairs={{0,1},{1,2},{2,3},{3,4},{4,5},{5,6},{6,7},{7,8},{8,9},{9,10},{10,1... | collective-permute-start | bytes 294920 | tf_op jit(solution)/shard_map/ppermute | solution.py:10
  140.0 6.2 %collective-permute-start.10 = (bf16[3,256,64]{1,2,0:T(8,128)(2,1)S(1)}, bf16[3,256,64]{1,2,0:T(8,128)(2,1)S(1)}, u32[]{:S(2)}, u32[]{:S(2)}) collective-permute-start(bf16[3,256,64]{1,2,0:T(8,128)(2,1)S(1)} %pad_maximum_fusion.1), channel_id=1, source_target_pairs={{1,0},{2,1},{3,2},{4,3},{5,4},{6,5},{7,6},{8,7},{9,8},{10,9},{11,1... | collective-permute-start | bytes 294920 | tf_op jit(solution)/shard_map/ppermute | solution.py:10
  143.6 10.1 %collective-permute-start.11 = (bf16[3,256,64]{1,2,0:T(8,128)(2,1)S(1)}, bf16[3,256,64]{1,2,0:T(8,128)(2,1)S(1)}, u32[]{:S(2)}, u32[]{:S(2)}) collective-permute-start(bf16[3,256,64]{1,2,0:T(8,128)(2,1)S(1)} %pad_maximum_fusion.1), channel_id=1, source_target_pairs={{2,0},{3,1},{4,2},{5,3},{6,4},{7,5},{8,6},{9,7},{10,8},{11,9},{12,... | collective-permute-start | bytes 294920 | tf_op jit(solution)/shard_map/ppermute | solution.py:10
  154.7 11.4 %collective-permute-start.12 = (bf16[3,256,64]{1,2,0:T(8,128)(2,1)S(1)}, bf16[3,256,64]{1,2,0:T(8,128)(2,1)S(1)}, u32[]{:S(2)}, u32[]{:S(2)}) collective-permute-start(bf16[3,256,64]{1,2,0:T(8,128)(2,1)S(1)} %pad_maximum_fusion.2), channel_id=1, source_target_pairs={{0,2},{1,3},{2,4},{3,5},{4,6},{5,7},{6,8},{7,9},{8,10},{9,11},{10,... | collective-permute-start | bytes 294920 | tf_op jit(solution)/shard_map/ppermute | solution.py:10
  156.6 9.5 %collective-permute-start.13 = (bf16[3,256,64]{1,2,0:T(8,128)(2,1)S(1)}, bf16[3,256,64]{1,2,0:T(8,128)(2,1)S(1)}, u32[]{:S(2)}, u32[]{:S(2)}) collective-permute-start(bf16[3,256,64]{1,2,0:T(8,128)(2,1)S(1)} %pad_maximum_fusion.2), channel_id=1, source_target_pairs={{0,1},{1,2},{2,3},{3,4},{4,5},{5,6},{6,7},{7,8},{8,9},{9,10},{10,1... | collective-permute-start | bytes 294920 | tf_op jit(solution)/shard_map/ppermute | solution.py:10
  158.5 7.7 %collective-permute-start.14 = (bf16[3,256,64]{1,2,0:T(8,128)(2,1)S(1)}, bf16[3,256,64]{1,2,0:T(8,128)(2,1)S(1)}, u32[]{:S(2)}, u32[]{:S(2)}) collective-permute-start(bf16[3,256,64]{1,2,0:T(8,128)(2,1)S(1)} %pad_maximum_fusion.2), channel_id=1, source_target_pairs={{1,0},{2,1},{3,2},{4,3},{5,4},{6,5},{7,6},{8,7},{9,8},{10,9},{11,1... | collective-permute-start | bytes 294920 | tf_op jit(solution)/shard_map/ppermute | solution.py:10
  162.2 10.1 %collective-permute-start.15 = (bf16[3,256,64]{1,2,0:T(8,128)(2,1)S(1)}, bf16[3,256,64]{1,2,0:T(8,128)(2,1)S(1)}, u32[]{:S(2)}, u32[]{:S(2)}) collective-permute-start(bf16[3,256,64]{1,2,0:T(8,128)(2,1)S(1)} %pad_maximum_fusion.2), channel_id=1, source_target_pairs={{2,0},{3,1},{4,2},{5,3},{6,4},{7,5},{8,6},{9,7},{10,8},{11,9},{12,... | collective-permute-start | bytes 294920 | tf_op jit(solution)/shard_map/ppermute | solution.py:10
Sparse Core Ops, SparseCore 0:
  8.9 31.7 all-gather.1
  86.8 26.0 reduce-scatter.3
where the time goes:
time: 181 us
  waiting for transfers between devices  65.8 us (36%)
  starting transfers between devices  45.6 us (25%)
  matrix products  28.6 us (16%)
  local copies, waits for them, and re-layouts  15.8 us (9%)
  between operations  13.9 us (8%)
  other arithmetic  11.1 us (6%)
    ppermute x16, starting transfers between devices, shifted(): return lax.ppermute(block, axis, route)  45.6 us
    unnamed x3, waiting for transfers between devices  25.9 us
    ppermute x16, waiting for transfers between devices, shifted(): return lax.ppermute(block, axis, route)  21.1 us
    all_gather x1, waiting for transfers between devices, on_device(): group_past = lax.all_gather(past, ('row', 'cur'), axis=0, tiled=True)  18.8 us
    dot_general x1, matrix products, on_device(): jnp.einsum('kij,skjr->skir', hist_tiles[0], picked, preferred_element_typ...  15.9 us
    gather x1, local copies, waits for them, and re-layouts, on_device(): picked = group_past[tile_cols[0][None, :], when]  11.7 us
    convert_element_type x1, other arithmetic, on_device(): terms_high = terms.astype(jnp.bfloat16)  8.06 us
    dot_general x1, matrix products, on_device(): jnp.einsum('gk,skir->gsir', onehot, terms_high, preferred_element_type=jn...  4.68 us
  transfers between devices with their start and end apart: 18, of which 5 were waited for; matrix products, arithmetic and copies ran while one was open for 28% of the time, Pallas kernels for 0%

commit v1 on v0

v1 whole, which is shorter than its diff:
```python
import functools

import jax
import jax.numpy as jnp
from jax import lax
from jax.experimental import pallas as pl
from jax.experimental.pallas import tpu as pltpu
from jax.sharding import PartitionSpec as P

BATCH = 8


def partner(me, distance, count):
    if count & (count - 1) == 0:
        return me ^ distance
    return (me + distance) % count


def rotated(block, axis, distance):
    count = lax.axis_size(axis)
    return lax.ppermute(block, axis, [(i, (i + distance) % count) for i in range(count)])


def shifted(block, axis, distance):
    count = lax.axis_size(axis)
    return lax.ppermute(block, axis, [(i, i + distance) for i in range(count) if 0 <= i + distance < count])


def swapped(block):
    return lax.ppermute(block, "cur", [(0, 1), (1, 0)])


def in_order(mine, theirs):
    lower = lax.axis_index("cur") == 0
    return jnp.stack([jnp.where(lower, mine, theirs), jnp.where(lower, theirs, mine)])


def halved(block):
    half = block.shape[-2] // 2
    core = lax.axis_index("cur")
    axis = block.ndim - 2
    mine = lax.dynamic_slice_in_dim(block, core * half, half, axis)
    others = lax.dynamic_slice_in_dim(block, (1 - core) * half, half, axis)
    return in_order(mine, swapped(others))


def history_kernel(first, count, kept, n_hist, n_row, n_chunks, *refs):
    pos, rows, cols, lags, scales = refs[:5]
    n_slots = 2 * n_row
    sources = refs[5 : 5 + n_slots * n_chunks]
    tiles = refs[5 + n_slots * n_chunks]
    outs = refs[6 + n_slots * n_chunks : 6 + n_slots * n_chunks + n_hist]
    held, weights, total, held_sem, weight_sem = refs[6 + n_slots * n_chunks + n_hist :]
    tile_count = tiles.shape[0]
    batches = tile_count // BATCH
    illum = outs[0].shape[0] // count

    copies = []
    for slot in range(n_slots):
        start = 0
        for chunk in range(n_chunks):
            source = sources[slot * n_chunks + chunk]
            size = source.shape[0]
            copies.append(
                pltpu.make_async_copy(source, held.at[slot, pl.ds(start, size)], held_sem.at[slot, chunk])
            )
            start += size
    for copy in copies:
        copy.start()

    def load(batch):
        at = pl.ds(batch * BATCH, BATCH)
        return pltpu.make_async_copy(tiles.at[at], weights.at[at], weight_sem.at[batch])

    for batch in range(batches):
        load(batch).start()
    total[...] = jnp.zeros_like(total)
    for copy in copies:
        copy.wait()

    def body(batch, carry):
        load(batch).wait()
        for inner in range(BATCH):
            tile = batch * BATCH + inner
            target = partner_index(rows[tile], pos[0], n_hist)
            column = cols[tile]
            away = lax.rem(pos[1] - lax.div(column, 2) + n_row, n_row)
            slot = jnp.where(lax.rem(column, 2) == pos[2], 0, n_row) + away
            start = pl.multiple_of((first - lags[tile] + kept) * illum, illum)
            x = held[slot, pl.ds(start, count * illum), :]
            y = lax.dot_general(
                x, weights[tile], (((1,), (1,)), ((), ())), preferred_element_type=jnp.float32
            )
            total[target] += y * scales[tile]
        return carry

    lax.fori_loop(0, batches, body, 0)
    for distance in range(n_hist):
        outs[distance][...] = total[distance].astype(outs[distance].dtype)


def partner_index(row, me, count):
    if count & (count - 1) == 0:
        return lax.bitwise_xor(row, me)
    return lax.rem(row - me + count, count)


def history_parts(sources, tiles, rows, cols, lags, scales, pos, first, count, kept, illum, n_hist, n_row):
    n_chunks = len(sources[0])
    size = tiles.shape[-1]
    held_rows = sum(chunk.shape[0] for chunk in sources[0])
    smem = pl.BlockSpec(memory_space=pltpu.SMEM)
    anywhere = pl.BlockSpec(memory_space=pl.ANY)
    flat = [chunk for slot in sources for chunk in slot]
    n_tiles = tiles.shape[0]
    return pl.pallas_call(
        functools.partial(history_kernel, first, count, kept, n_hist, n_row, n_chunks),
        out_shape=[
            jax.ShapeDtypeStruct((count * illum, size), jnp.float32 if d == 0 else jnp.bfloat16)
            for d in range(n_hist)
        ],
        in_specs=[smem] * 5 + [anywhere] * (len(flat) + 1),
        out_specs=[pl.BlockSpec(memory_space=pltpu.VMEM)] * n_hist,
        scratch_shapes=[
            pltpu.VMEM((len(sources), held_rows, size), jnp.bfloat16),
            pltpu.VMEM((n_tiles, size, size), jnp.bfloat16),
            pltpu.VMEM((n_hist, count * illum, size), jnp.float32),
            pltpu.SemaphoreType.DMA((len(sources), n_chunks)),
            pltpu.SemaphoreType.DMA((n_tiles // BATCH,)),
        ],
        compiler_params=pltpu.CompilerParams(vmem_limit_bytes=48 << 20),
        cost_estimate=pl.CostEstimate(
            flops=2 * n_tiles * count * illum * size * size,
            bytes_accessed=2 * n_tiles * size * size,
            transcendentals=0,
        ),
    )(pos, rows, cols, lags, scales, *flat, tiles)


def on_device(
    incident, past, hist_tiles, tile_rows, tile_cols, tile_lags, tile_scales, near_tiles, inverses
):
    n_hist, n_row = lax.axis_size("hist"), lax.axis_size("row")
    core = lax.axis_index("cur")
    steps, _, size, illum = incident.shape
    kept = past.shape[1]
    spans = near_tiles.shape[1]
    offsets = near_tiles.shape[2]
    chips = ("hist", "row")
    pos = jnp.stack([lax.axis_index("hist"), lax.axis_index("row"), core]).astype(jnp.int32)
    incident = jnp.swapaxes(incident[:, 0], 1, 2)
    past = jnp.swapaxes(past[0], 1, 2)
    early = past[: kept - 3].reshape((kept - 3) * illum, size)
    late = past[kept - 3 :].reshape(3 * illum, size)

    along = [[early, late]]
    for distance in range(1, n_row):
        along.append([rotated(early, "row", distance)])
    for distance in range(1, n_row):
        along[distance].append(rotated(late, "row", distance))
    across = [[swapped(chunk) for chunk in slot] for slot in along]
    sources = along + across

    tables = (tile_rows[0], tile_cols[0], tile_lags[0], tile_scales[0])

    def reduced(parts):
        total = parts[0]
        for distance in range(1, n_hist):
            route = [(i, partner(i, distance, n_hist)) for i in range(n_hist)]
            total = total + lax.ppermute(parts[distance], "hist", route).astype(jnp.float32)
        return halved(total.reshape(-1, illum, size))

    parts = history_parts(
        [slot[:1] for slot in sources], hist_tiles[0], *tables, pos, 0, 1, kept, illum, n_hist, n_row
    )
    first_history = reduced(parts)
    parts = history_parts(
        sources, hist_tiles[0], *tables, pos, 1, steps - 1, kept, illum, n_hist, n_row
    )
    later_history = reduced(parts)

    near = in_order(near_tiles[0], swapped(near_tiles[0]))
    inverse = in_order(inverses[0], swapped(inverses[0]))
    own = halved(jnp.concatenate([incident, past[kept - 3 :]], axis=0))
    incident, window = own[:, :steps].astype(jnp.float32), own[:, steps:]

    def neighbours(block):
        return jnp.concatenate([shifted(block, chips, 1), block, shifted(block, chips, -1)], axis=0)

    def coupled(sources, lag):
        return jnp.stack(
            [
                jnp.einsum(
                    "orj,oij->ri",
                    sources[q : q + offsets],
                    near[q, lag - 1],
                    preferred_element_type=jnp.float32,
                )
                for q in range(2)
            ]
        )

    around = neighbours(window)
    held = {step - 3: around[:, step] for step in range(3)}
    made = []
    for step in range(steps):
        history = first_history[:, 0] if step == 0 else later_history[:, step - 1]
        ready = incident[:, step] - history
        for lag in range(spans, 0, -1):
            ready = ready - coupled(held[step - lag], lag)
        rhs = ready.astype(jnp.bfloat16)
        fresh = jnp.einsum(
            "qrj,qij->qri", rhs, inverse, preferred_element_type=jnp.float32
        ).astype(jnp.bfloat16)
        made.append(fresh)
        if step + 1 < steps:
            held[step] = neighbours(fresh)

    made = jnp.stack(made, axis=1)
    lower = core == 0
    mine = jnp.where(lower, made[0], made[1])
    other = swapped(jnp.where(lower, made[1], made[0]))
    whole = jnp.concatenate(
        [jnp.where(lower, mine, other), jnp.where(lower, other, mine)], axis=1
    )
    return jnp.swapaxes(whole, 1, 2)[:, None]


def solution(mesh):
    every = ("hist", "row", "cur")
    placed = (
        P(None, every, None, None),
        P(every, None, None, None),
        P(every, None, None, None),
        P(every, None),
        P(every, None),
        P(every, None),
        P(every, None),
        P(every, None, None, None, None),
        P(every, None, None),
    )
    return jax.shard_map(
        on_device,
        mesh=mesh,
        in_specs=placed,
        out_specs=P(None, every, None, None),
        check_vma=False,
    )
```

time: 181 us -> 110 us (0.61)
  the two profiles are of different devices: /device:TPU:26 before, /device:TPU:5 now
where the time goes in v1:
time: 110 us; the launch traced here: 109 us
  starting transfers between devices  53.2 us (48%)
  waiting for transfers between devices  25.6 us (23%)
  Pallas kernels  16.4 us (15%)
  matrix products  8.71 us (8%)
  other arithmetic  3.04 us (3%)
  local copies, waits for them, and re-layouts  1.97 us (2%)
    ppermute x8, starting transfers between devices, shifted(): lax.ppermute(block, axis, [(i, i + distance) for i in range(count) if 0 <...  23.9 us
    ppermute x14, starting transfers between devices, swapped(): return lax.ppermute(block, 'cur', [(0, 1), (1, 0)])  18.5 us
    pallas_call x2, Pallas kernels, history_parts(): pl.pallas_call(functools.partial(history_kernel, first, count, kept, n_hi...  16.4 us
    ppermute x8, waiting for transfers between devices, shifted(): lax.ppermute(block, axis, [(i, i + distance) for i in range(count) if 0 <...  13.9 us
    ppermute x6, waiting for transfers between devices, rotated(): lax.ppermute(block, axis, [(i, (i + distance) % count) for i in range(cou...  8.83 us
    dot_general x24, matrix products, coupled(): jnp.einsum('orj,oij->ri', sources[q:q + offsets], near[q, lag - 1], prefe...  7.79 us
    ppermute x6, starting transfers between devices, reduced(): lax.ppermute(parts[distance], 'hist', route).astype(jnp.float32)  5.43 us
    ppermute x6, starting transfers between devices, rotated(): lax.ppermute(block, axis, [(i, (i + distance) % count) for i in range(cou...  5.3 us
  transfers between devices with their start and end apart: 34, of which 8 were waited for; matrix products, arithmetic and copies ran while one was open for 4% of the time, Pallas kernels for 15%

profile of v1, /device:TPU:5, one launch (start us, length us, event | category | flops | bytes accessed | tf_op | source)
XLA Modules:
  0.0 109.2 jit_solution(945355800695976839)
XLA Ops:
  2.6 3.3 %collective-permute-start.18 = (bf16[192,256]{1,0:T(8,128)(2,1)S(1)}, bf16[192,256]{1,0:T(8,128)(2,1)S(1)}, u32[]{:S(2)}, u32[]{:S(2)}) collective-permute-start(bf16[192,256]{1,0:T(8,128)(2,1)S(1)} %bitcast.273), channel_id=1, source_target_pairs={{0,6},{2,0},{4,2},{6,4},{1,7},{3,1},{5,3},{7,5},{8,14},{10,8},{12,... | collective-permute-start | bytes 294920 | tf_op jit(solution)/shard_map/ppermute | solution.py:21
  10.5 4.8 %collective-permute-done.17.refs_10_ = bf16[192,256]{1,0:T(8,128)(2,1)S(1)} collective-permute-done((bf16[192,256]{1,0:T(8,128)(2,1)S(1)}, bf16[192,256]{1,0:T(8,128)(2,1)S(1)}, u32[]{:S(2)}, u32[]{:S(2)}) %collective-permute-start.17) | collective-permute-done | bytes 98336 | tf_op jit(solution)/shard_map/ppermute | solution.py:21
  15.2 1.2 %collective-permute-start.2 = (bf16[320,256]{1,0:T(8,128)(2,1)S(1)}, bf16[320,256]{1,0:T(8,128)(2,1)S(1)}, u32[]{:S(2)}, u32[]{:S(2)}) collective-permute-start(bf16[320,256]{1,0:T(8,128)(2,1)S(1)} %bitcast.280), channel_id=1, source_target_pairs={{0,4},{2,6},{4,0},{6,2},{1,5},{3,7},{5,1},{7,3},{8,12},{10,14},{12... | collective-permute-start | bytes 491528 | tf_op jit(solution)/shard_map/ppermute | solution.py:21
  16.8 5.7 %collective-permute-start.13 = (bf16[2,3,32,256]{3,2,0,1:T(8,128)(2,1)S(1)}, bf16[2,3,32,256]{3,2,0,1:T(8,128)(2,1)S(1)}, u32[]{:S(2)}, u32[]{:S(2)}) collective-permute-start(bf16[2,3,32,256]{3,2,0,1:T(8,128)(2,1)S(1)} %pad_maximum_fusion.3), channel_id=1, source_target_pairs={{2,0},{4,2},{6,4},{8,6},{10,8},{12,10},{14,12},{16,14},{18,16},{20... | collective-permute-start | bytes 294920 | tf_op jit(solution)/shard_map/ppermute | solution.py:26
  22.6 1.9 %collective-permute-start.12 = (bf16[2,3,32,256]{3,2,0,1:T(8,128)(2,1)S(1)}, bf16[2,3,32,256]{3,2,0,1:T(8,128)(2,1)S(1)}, u32[]{:S(2)}, u32[]{:S(2)}) collective-permute-start(bf16[2,3,32,256]{3,2,0,1:T(8,128)(2,1)S(1)} %pad_maximum_fusion.3), channel_id=1, source_target_pairs={{0,2},{2,4},{4,6},{6,8},{8,10},{10,12},{12,14},{14,16},{16,18},{18... | collective-permute-start | bytes 294920 | tf_op jit(solution)/shard_map/ppermute | solution.py:26
  24.5 4.1 %collective-permute-done.2.refs_7_.refs_9_ = bf16[320,256]{1,0:T(8,128)(2,1)S(1)} collective-permute-done((bf16[320,256]{1,0:T(8,128)(2,1)S(1)}, bf16[320,256]{1,0:T(8,128)(2,1)S(1)}, u32[]{:S(2)}, u32[]{:S(2)}) %collective-permute-start.2) | collective-permute-done | bytes 163872 | tf_op jit(solution)/shard_map/ppermute | solution.py:21
  28.6 3.8 %collective-permute-start.7 = (bf16[320,256]{1,0:T(8,128)(2,1)S(1)}, bf16[320,256]{1,0:T(8,128)(2,1)S(1)}, u32[]{:S(2)}, u32[]{:S(2)}) collective-permute-start(bf16[320,256]{1,0:T(8,128)(2,1)S(1)} %collective-permute-done.3.refs_8_.refs_11_), channel_id=1, source_target_pairs={{0,1},{1,0},{2,3},{3,2},{4,5},{5,4},{6,7},{7,6},{8,9},{9,8},{10,11... | collective-permute-start | bytes 491528 | tf_op jit(solution)/shard_map/ppermute | solution.py:30
  32.9 2.2 %collective-permute-start.19 = (bf16[192,256]{1,0:T(8,128)(2,1)S(1)}, bf16[192,256]{1,0:T(8,128)(2,1)S(1)}, u32[]{:S(2)}, u32[]{:S(2)}) collective-permute-start(bf16[192,256]{1,0:T(8,128)(2,1)S(1)} %bitcast.276), channel_id=1, source_target_pairs={{0,1},{1,0},{2,3},{3,2},{4,5},{5,4},{6,7},{7,6},{8,9},{9,8},{10,11... | collective-permute-start | bytes 294920 | tf_op jit(solution)/shard_map/ppermute | solution.py:30
  35.8 7.3 %shard_map.91 = (f32[64,256]{1,0:T(8,128)S(1)}, bf16[64,256]{1,0:T(8,128)(2,1)S(1)}, bf16[64,256]{1,0:T(8,128)(2,1)S(1)}, bf16[64,256]{1,0:T(8,128)(2,1)S(1)}) custom-call(s32[3]{0:T(128)S(1)} %pad_add_fusion.refs_0_, s32[64]{0:T(128)S(1)} %bitcast.284, s32[64]{0:T(128)S(1)} %bitcast.286, s32[64]{0:T(128)S(1)} %bitcast.288, f32[64]{0:T(128)S(1)} %bitcast.290, ...), custom_call_target="tpu_custom_call" | custom-call | flops 536870912 | bytes 8388608 | tf_op jit(solution)/shard_map/pallas_call | solution.py:116
  43.7 2.1 %collective-permute-start.10 = (bf16[64,256]{1,0:T(8,128)(2,1)S(1)}, bf16[64,256]{1,0:T(8,128)(2,1)S(1)}, u32[]{:S(2)}, u32[]{:S(2)}) collective-permute-start(bf16[64,256]{1,0:T(8,128)(2,1)S(1)} %get-tuple-element.16), channel_id=1, source_target_pairs={{0,24},{8,16},{16,8},{24,0},{1,25},{9,17},{17,9},{25,1},{2,26},{10... | collective-permute-start | bytes 98312 | tf_op jit(solution)/shard_map/ppermute | solution.py:170
  45.8 9.1 %shard_map.92 = (f32[192,256]{1,0:T(8,128)S(1)}, bf16[192,256]{1,0:T(8,128)(2,1)S(1)}, bf16[192,256]{1,0:T(8,128)(2,1)S(1)}, bf16[192,256]{1,0:T(8,128)(2,1)S(1)}) custom-call(s32[3]{0:T(128)S(1)} %pad_add_fusion.refs_0_, s32[64]{0:T(128)S(1)} %bitcast.285, s32[64]{0:T(128)S(1)} %bitcast.287, s32[64]{0:T(128)S(1)} %bitcast.289, f32[64]{0:T(128)S(1)} %bitcast.291, ...), custom_call_target="tpu_custom_call" | custom-call | flops 1610612736 | bytes 8388608 | tf_op jit(solution)/shard_map/pallas_call | solution.py:116
  55.5 2.1 %collective-permute-start.25 = (bf16[192,256]{1,0:T(8,128)(2,1)S(1)}, bf16[192,256]{1,0:T(8,128)(2,1)S(1)}, u32[]{:S(2)}, u32[]{:S(2)}) collective-permute-start(bf16[192,256]{1,0:T(8,128)(2,1)S(1)} %get-tuple-element.20), channel_id=1, source_target_pairs={{0,24},{8,16},{16,8},{24,0},{1,25},{9,17},{17,9},{25,1},{2,26},{10... | collective-permute-start | bytes 294920 | tf_op jit(solution)/shard_map/ppermute | solution.py:170
  57.7 2.2 %collective-permute-start.11 = (f32[1,32,256]{2,1,0:T(8,128)S(1)}, f32[1,32,256]{2,1,0:T(8,128)S(1)}, u32[]{:S(2)}, u32[]{:S(2)}) collective-permute-start(f32[1,32,256]{2,1,0:T(8,128)S(1)} %dynamic-slice_bitcast_fusion), channel_id=1, source_target_pairs={{0,1},{1,0},{2,3},{3,2},{4,5},{5,4},{6,7},{7,6},{8,9},{9,8},{10,11... | collective-permute-start | bytes 98312 | tf_op jit(solution)/shard_map/ppermute | solution.py:30
  60.9 2.4 %collective-permute-start.26 = (f32[3,32,256]{2,1,0:T(8,128)S(1)}, f32[3,32,256]{2,1,0:T(8,128)S(1)}, u32[]{:S(2)}, u32[]{:S(2)}) collective-permute-start(f32[3,32,256]{2,1,0:T(8,128)S(1)} %constant_dynamic-slice_fusion), channel_id=1, source_target_pairs={{0,1},{1,0},{2,3},{3,2},{4,5},{5,4},{6,7},{7,6},{8,9},{9,8},{10,11... | collective-permute-start | bytes 294920 | tf_op jit(solution)/shard_map/ppermute | solution.py:30
  68.5 3.8 %collective-permute-start.28 = (bf16[2,32,256]{2,1,0:T(8,128)(2,1)S(1)}, bf16[2,32,256]{2,1,0:T(8,128)(2,1)S(1)}, u32[]{:S(2)}, u32[]{:S(2)}) collective-permute-start(bf16[2,32,256]{2,1,0:T(8,128)(2,1)S(1)} %convolution_convert_fusion.3), channel_id=1, source_target_pairs={{2,0},{4,2},{6,4},{8,6},{10,8},{12,10},{14,12},{16,14},{18,16},{20... | collective-permute-start | bytes 98312 | tf_op jit(solution)/shard_map/ppermute | solution.py:26
  72.2 1.9 %collective-permute-start.27 = (bf16[2,32,256]{2,1,0:T(8,128)(2,1)S(1)}, bf16[2,32,256]{2,1,0:T(8,128)(2,1)S(1)}, u32[]{:S(2)}, u32[]{:S(2)}) collective-permute-start(bf16[2,32,256]{2,1,0:T(8,128)(2,1)S(1)} %convolution_convert_fusion.3), channel_id=1, source_target_pairs={{0,2},{2,4},{4,6},{6,8},{8,10},{10,12},{12,14},{14,16},{16,18},{18... | collective-permute-start | bytes 98312 | tf_op jit(solution)/shard_map/ppermute | solution.py:26
  74.5 6.0 %collective-permute-done.27 = bf16[2,32,256]{2,1,0:T(8,128)(2,1)S(1)} collective-permute-done((bf16[2,32,256]{2,1,0:T(8,128)(2,1)S(1)}, bf16[2,32,256]{2,1,0:T(8,128)(2,1)S(1)}, u32[]{:S(2)}, u32[]{:S(2)}) %collective-permute-start.27) | collective-permute-done | bytes 32800 | tf_op jit(solution)/shard_map/ppermute | solution.py:26
  81.4 1.9 %collective-permute-start.30 = (bf16[2,32,256]{2,1,0:T(8,128)(2,1)S(1)}, bf16[2,32,256]{2,1,0:T(8,128)(2,1)S(1)}, u32[]{:S(2)}, u32[]{:S(2)}) collective-permute-start(bf16[2,32,256]{2,1,0:T(8,128)(2,1)S(1)} %convolution_convert_fusion.2), channel_id=1, source_target_pairs={{2,0},{4,2},{6,4},{8,6},{10,8},{12,10},{14,12},{16,14},{18,16},{20... | collective-permute-start | bytes 98312 | tf_op jit(solution)/shard_map/ppermute | solution.py:26
  83.3 3.4 %collective-permute-start.29 = (bf16[2,32,256]{2,1,0:T(8,128)(2,1)S(1)}, bf16[2,32,256]{2,1,0:T(8,128)(2,1)S(1)}, u32[]{:S(2)}, u32[]{:S(2)}) collective-permute-start(bf16[2,32,256]{2,1,0:T(8,128)(2,1)S(1)} %convolution_convert_fusion.2), channel_id=1, source_target_pairs={{0,2},{2,4},{4,6},{6,8},{8,10},{10,12},{12,14},{14,16},{16,18},{18... | collective-permute-start | bytes 98312 | tf_op jit(solution)/shard_map/ppermute | solution.py:26
  88.0 3.6 %collective-permute-done.29 = bf16[2,32,256]{2,1,0:T(8,128)(2,1)S(1)} collective-permute-done((bf16[2,32,256]{2,1,0:T(8,128)(2,1)S(1)}, bf16[2,32,256]{2,1,0:T(8,128)(2,1)S(1)}, u32[]{:S(2)}, u32[]{:S(2)}) %collective-permute-start.29) | collective-permute-done | bytes 32800 | tf_op jit(solution)/shard_map/ppermute | solution.py:26
  92.4 2.0 %collective-permute-start.32 = (bf16[2,32,256]{2,1,0:T(8,128)(2,1)S(1)}, bf16[2,32,256]{2,1,0:T(8,128)(2,1)S(1)}, u32[]{:S(2)}, u32[]{:S(2)}) collective-permute-start(bf16[2,32,256]{2,1,0:T(8,128)(2,1)S(1)} %convolution_convert_fusion.1), channel_id=1, source_target_pairs={{2,0},{4,2},{6,4},{8,6},{10,8},{12,10},{14,12},{16,14},{18,16},{20... | collective-permute-start | bytes 98312 | tf_op jit(solution)/shard_map/ppermute | solution.py:26
  94.4 3.3 %collective-permute-start.31 = (bf16[2,32,256]{2,1,0:T(8,128)(2,1)S(1)}, bf16[2,32,256]{2,1,0:T(8,128)(2,1)S(1)}, u32[]{:S(2)}, u32[]{:S(2)}) collective-permute-start(bf16[2,32,256]{2,1,0:T(8,128)(2,1)S(1)} %convolution_convert_fusion.1), channel_id=1, source_target_pairs={{0,2},{2,4},{4,6},{6,8},{8,10},{10,12},{12,14},{14,16},{16,18},{18... | collective-permute-start | bytes 98312 | tf_op jit(solution)/shard_map/ppermute | solution.py:26
  98.3 4.3 %collective-permute-done.31 = bf16[2,32,256]{2,1,0:T(8,128)(2,1)S(1)} collective-permute-done((bf16[2,32,256]{2,1,0:T(8,128)(2,1)S(1)}, bf16[2,32,256]{2,1,0:T(8,128)(2,1)S(1)}, u32[]{:S(2)}, u32[]{:S(2)}) %collective-permute-start.31) | collective-permute-done | bytes 32800 | tf_op jit(solution)/shard_map/ppermute | solution.py:26
  103.6 4.1 %collective-permute-start.33 = (bf16[4,32,256]{2,1,0:T(8,128)(2,1)S(1)}, bf16[4,32,256]{2,1,0:T(8,128)(2,1)S(1)}, u32[]{:S(2)}, u32[]{:S(2)}) collective-permute-start(bf16[4,32,256]{2,1,0:T(8,128)(2,1)S(1)} %fusion.5), channel_id=1, source_target_pairs={{0,1},{1,0},{2,3},{3,2},{4,5},{5,4},{6,7},{7,6},{8,9},{9,8},{10,11... | collective-permute-start | bytes 196616 | tf_op jit(solution)/shard_map/ppermute | solution.py:30
  (106 shorter events, 22.5 us)
Async XLA Ops:
  1.9 7.6 %collective-permute-start = (bf16[7,32,256]{2,1,0:T(8,128)(2,1)S(1)}, bf16[7,32,256]{2,1,0:T(8,128)(2,1)S(1)}, u32[]{:S(2)}, u32[]{:S(2)}) collective-permute-start(bf16[7,32,256]{2,1,0:T(8,128)(2,1)S(1)} %fusion.3), channel_id=1, source_target_pairs={{0,1},{1,0},{2,3},{3,2},{4,5},{5,4},{6,7},{7,6},{8,9},{9,8},{10,11... | collective-permute-start | bytes 344072 | tf_op jit(solution)/shard_map/ppermute | solution.py:30
  5.9 9.3 %collective-permute-start.17 = (bf16[192,256]{1,0:T(8,128)(2,1)S(1)}, bf16[192,256]{1,0:T(8,128)(2,1)S(1)}, u32[]{:S(2)}, u32[]{:S(2)}) collective-permute-start(bf16[192,256]{1,0:T(8,128)(2,1)S(1)} %bitcast.274), channel_id=1, source_target_pairs={{0,4},{2,6},{4,0},{6,2},{1,5},{3,7},{5,1},{7,3},{8,12},{10,14},{12... | collective-permute-start | bytes 294920 | tf_op jit(solution)/shard_map/ppermute | solution.py:21
  5.9 9.3 %collective-permute-start.16 = (bf16[192,256]{1,0:T(8,128)(2,1)S(1)}, bf16[192,256]{1,0:T(8,128)(2,1)S(1)}, u32[]{:S(2)}, u32[]{:S(2)}) collective-permute-start(bf16[192,256]{1,0:T(8,128)(2,1)S(1)} %bitcast.275), channel_id=1, source_target_pairs={{0,2},{2,4},{4,6},{6,0},{1,3},{3,5},{5,7},{7,1},{8,10},{10,12},{12... | collective-permute-start | bytes 294920 | tf_op jit(solution)/shard_map/ppermute | solution.py:21
  6.4 10.1 %collective-permute-start.15 = (bf16[256,256]{1,0:T(8,128)(2,1)}, bf16[256,256]{1,0:T(8,128)(2,1)S(1)}, u32[]{:S(2)}, u32[]{:S(2)}) collective-permute-start(bf16[256,256]{1,0:T(8,128)(2,1)} %bitcast.301), channel_id=1, source_target_pairs={{0,1},{1,0},{2,3},{3,2},{4,5},{5,4},{6,7},{7,6},{8,9},{9,8},{10,11... | collective-permute-start | bytes 393224 | tf_op jit(solution)/shard_map/ppermute | solution.py:30
  8.3 8.5 %collective-permute-start.4 = (bf16[320,256]{1,0:T(8,128)(2,1)S(1)}, bf16[320,256]{1,0:T(8,128)(2,1)S(1)}, u32[]{:S(2)}, u32[]{:S(2)}) collective-permute-start(bf16[320,256]{1,0:T(8,128)(2,1)S(1)} %bitcast.278), channel_id=1, source_target_pairs={{0,1},{1,0},{2,3},{3,2},{4,5},{5,4},{6,7},{7,6},{8,9},{9,8},{10,11... | collective-permute-start | bytes 491528 | tf_op jit(solution)/shard_map/ppermute | solution.py:30
  9.5 54.7 %collective-permute-start.14 = (bf16[3,5,256,256]{3,2,1,0:T(8,128)(2,1)}, bf16[3,5,256,256]{3,2,1,0:T(8,128)(2,1)S(1)}, u32[]{:S(2)}, u32[]{:S(2)}) collective-permute-start(bf16[3,5,256,256]{3,2,1,0:T(8,128)(2,1)} %bitcast.294), channel_id=1, source_target_pairs={{0,1},{1,0},{2,3},{3,2},{4,5},{5,4},{6,7},{7,6},{8,9},{9,8},{10,11... | collective-permute-start | bytes 5898248 | tf_op jit(solution)/shard_map/ppermute | solution.py:30
  15.2 7.3 %collective-permute-start.3 = (bf16[320,256]{1,0:T(8,128)(2,1)S(1)}, bf16[320,256]{1,0:T(8,128)(2,1)S(1)}, u32[]{:S(2)}, u32[]{:S(2)}) collective-permute-start(bf16[320,256]{1,0:T(8,128)(2,1)S(1)} %bitcast.279), channel_id=1, source_target_pairs={{0,6},{2,0},{4,2},{6,4},{1,7},{3,1},{5,3},{7,5},{8,14},{10,8},{12,... | collective-permute-start | bytes 491528 | tf_op jit(solution)/shard_map/ppermute | solution.py:21
  15.2 13.3 %collective-permute-start.2 = (bf16[320,256]{1,0:T(8,128)(2,1)S(1)}, bf16[320,256]{1,0:T(8,128)(2,1)S(1)}, u32[]{:S(2)}, u32[]{:S(2)}) collective-permute-start(bf16[320,256]{1,0:T(8,128)(2,1)S(1)} %bitcast.280), channel_id=1, source_target_pairs={{0,4},{2,6},{4,0},{6,2},{1,5},{3,7},{5,1},{7,3},{8,12},{10,14},{12... | collective-permute-start | bytes 491528 | tf_op jit(solution)/shard_map/ppermute | solution.py:21
  16.4 15.9 %collective-permute-start.1 = (bf16[320,256]{1,0:T(8,128)(2,1)S(1)}, bf16[320,256]{1,0:T(8,128)(2,1)S(1)}, u32[]{:S(2)}, u32[]{:S(2)}) collective-permute-start(bf16[320,256]{1,0:T(8,128)(2,1)S(1)} %bitcast.281), channel_id=1, source_target_pairs={{0,2},{2,4},{4,6},{6,0},{1,3},{3,5},{5,7},{7,1},{8,10},{10,12},{12... | collective-permute-start | bytes 491528 | tf_op jit(solution)/shard_map/ppermute | solution.py:21
  16.8 15.6 %collective-permute-start.13 = (bf16[2,3,32,256]{3,2,0,1:T(8,128)(2,1)S(1)}, bf16[2,3,32,256]{3,2,0,1:T(8,128)(2,1)S(1)}, u32[]{:S(2)}, u32[]{:S(2)}) collective-permute-start(bf16[2,3,32,256]{3,2,0,1:T(8,128)(2,1)S(1)} %pad_maximum_fusion.3), channel_id=1, source_target_pairs={{2,0},{4,2},{6,4},{8,6},{10,8},{12,10},{14,12},{16,14},{18,16},{20... | collective-permute-start | bytes 294920 | tf_op jit(solution)/shard_map/ppermute | solution.py:26
  22.6 10.3 %collective-permute-start.12 = (bf16[2,3,32,256]{3,2,0,1:T(8,128)(2,1)S(1)}, bf16[2,3,32,256]{3,2,0,1:T(8,128)(2,1)S(1)}, u32[]{:S(2)}, u32[]{:S(2)}) collective-permute-start(bf16[2,3,32,256]{3,2,0,1:T(8,128)(2,1)S(1)} %pad_maximum_fusion.3), channel_id=1, source_target_pairs={{0,2},{2,4},{4,6},{6,8},{8,10},{10,12},{12,14},{14,16},{16,18},{18... | collective-permute-start | bytes 294920 | tf_op jit(solution)/shard_map/ppermute | solution.py:26
  28.6 6.6 %collective-permute-start.7 = (bf16[320,256]{1,0:T(8,128)(2,1)S(1)}, bf16[320,256]{1,0:T(8,128)(2,1)S(1)}, u32[]{:S(2)}, u32[]{:S(2)}) collective-permute-start(bf16[320,256]{1,0:T(8,128)(2,1)S(1)} %collective-permute-done.3.refs_8_.refs_11_), channel_id=1, source_target_pairs={{0,1},{1,0},{2,3},{3,2},{4,5},{5,4},{6,7},{7,6},{8,9},{9,8},{10,11... | collective-permute-start | bytes 491528 | tf_op jit(solution)/shard_map/ppermute | solution.py:30
  32.9 10.2 %collective-permute-start.19 = (bf16[192,256]{1,0:T(8,128)(2,1)S(1)}, bf16[192,256]{1,0:T(8,128)(2,1)S(1)}, u32[]{:S(2)}, u32[]{:S(2)}) collective-permute-start(bf16[192,256]{1,0:T(8,128)(2,1)S(1)} %bitcast.276), channel_id=1, source_target_pairs={{0,1},{1,0},{2,3},{3,2},{4,5},{5,4},{6,7},{7,6},{8,9},{9,8},{10,11... | collective-permute-start | bytes 294920 | tf_op jit(solution)/shard_map/ppermute | solution.py:30
  35.1 8.3 %collective-permute-start.22 = (bf16[192,256]{1,0:T(8,128)(2,1)S(1)}, bf16[192,256]{1,0:T(8,128)(2,1)S(1)}, u32[]{:S(2)}, u32[]{:S(2)}) collective-permute-start(bf16[192,256]{1,0:T(8,128)(2,1)S(1)} %collective-permute-done.18.refs_12_), channel_id=1, source_target_pairs={{0,1},{1,0},{2,3},{3,2},{4,5},{5,4},{6,7},{7,6},{8,9},{9,8},{10,11... | collective-permute-start | bytes 294920 | tf_op jit(solution)/shard_map/ppermute | solution.py:30
  35.1 8.6 %collective-permute-start.21 = (bf16[192,256]{1,0:T(8,128)(2,1)S(1)}, bf16[192,256]{1,0:T(8,128)(2,1)S(1)}, u32[]{:S(2)}, u32[]{:S(2)}) collective-permute-start(bf16[192,256]{1,0:T(8,128)(2,1)S(1)} %collective-permute-done.17.refs_10_), channel_id=1, source_target_pairs={{0,1},{1,0},{2,3},{3,2},{4,5},{5,4},{6,7},{7,6},{8,9},{9,8},{10,11... | collective-permute-start | bytes 294920 | tf_op jit(solution)/shard_map/ppermute | solution.py:30
  35.6 10.2 %collective-permute-start.20 = (bf16[192,256]{1,0:T(8,128)(2,1)S(1)}, bf16[192,256]{1,0:T(8,128)(2,1)S(1)}, u32[]{:S(2)}, u32[]{:S(2)}) collective-permute-start(bf16[192,256]{1,0:T(8,128)(2,1)S(1)} %collective-permute-done.16.refs_8_), channel_id=1, source_target_pairs={{0,1},{1,0},{2,3},{3,2},{4,5},{5,4},{6,7},{7,6},{8,9},{9,8},{10,11... | collective-permute-start | bytes 294920 | tf_op jit(solution)/shard_map/ppermute | solution.py:30
  43.1 12.2 %collective-permute-start.8 = (bf16[64,256]{1,0:T(8,128)(2,1)S(1)}, bf16[64,256]{1,0:T(8,128)(2,1)S(1)}, u32[]{:S(2)}, u32[]{:S(2)}) collective-permute-start(bf16[64,256]{1,0:T(8,128)(2,1)S(1)} %get-tuple-element.14), channel_id=1, source_target_pairs={{0,8},{8,0},{16,24},{24,16},{1,9},{9,1},{17,25},{25,17},{2,10},{10... | collective-permute-start | bytes 98312 | tf_op jit(solution)/shard_map/ppermute | solution.py:170
  43.5 12.1 %collective-permute-start.9 = (bf16[64,256]{1,0:T(8,128)(2,1)S(1)}, bf16[64,256]{1,0:T(8,128)(2,1)S(1)}, u32[]{:S(2)}, u32[]{:S(2)}) collective-permute-start(bf16[64,256]{1,0:T(8,128)(2,1)S(1)} %get-tuple-element.15), channel_id=1, source_target_pairs={{0,16},{8,24},{16,0},{24,8},{1,17},{9,25},{17,1},{25,9},{2,18},{10... | collective-permute-start | bytes 98312 | tf_op jit(solution)/shard_map/ppermute | solution.py:170
  43.7 14.0 %collective-permute-start.10 = (bf16[64,256]{1,0:T(8,128)(2,1)S(1)}, bf16[64,256]{1,0:T(8,128)(2,1)S(1)}, u32[]{:S(2)}, u32[]{:S(2)}) collective-permute-start(bf16[64,256]{1,0:T(8,128)(2,1)S(1)} %get-tuple-element.16), channel_id=1, source_target_pairs={{0,24},{8,16},{16,8},{24,0},{1,25},{9,17},{17,9},{25,1},{2,26},{10... | collective-permute-start | bytes 98312 | tf_op jit(solution)/shard_map/ppermute | solution.py:170
  68.5 6.0 %collective-permute-start.28 = (bf16[2,32,256]{2,1,0:T(8,128)(2,1)S(1)}, bf16[2,32,256]{2,1,0:T(8,128)(2,1)S(1)}, u32[]{:S(2)}, u32[]{:S(2)}) collective-permute-start(bf16[2,32,256]{2,1,0:T(8,128)(2,1)S(1)} %convolution_convert_fusion.3), channel_id=1, source_target_pairs={{2,0},{4,2},{6,4},{8,6},{10,8},{12,10},{14,12},{16,14},{18,16},{20... | collective-permute-start | bytes 98312 | tf_op jit(solution)/shard_map/ppermute | solution.py:26
  72.2 8.3 %collective-permute-start.27 = (bf16[2,32,256]{2,1,0:T(8,128)(2,1)S(1)}, bf16[2,32,256]{2,1,0:T(8,128)(2,1)S(1)}, u32[]{:S(2)}, u32[]{:S(2)}) collective-permute-start(bf16[2,32,256]{2,1,0:T(8,128)(2,1)S(1)} %convolution_convert_fusion.3), channel_id=1, source_target_pairs={{0,2},{2,4},{4,6},{6,8},{8,10},{10,12},{12,14},{14,16},{16,18},{18... | collective-permute-start | bytes 98312 | tf_op jit(solution)/shard_map/ppermute | solution.py:26
  81.4 6.6 %collective-permute-start.30 = (bf16[2,32,256]{2,1,0:T(8,128)(2,1)S(1)}, bf16[2,32,256]{2,1,0:T(8,128)(2,1)S(1)}, u32[]{:S(2)}, u32[]{:S(2)}) collective-permute-start(bf16[2,32,256]{2,1,0:T(8,128)(2,1)S(1)} %convolution_convert_fusion.2), channel_id=1, source_target_pairs={{2,0},{4,2},{6,4},{8,6},{10,8},{12,10},{14,12},{16,14},{18,16},{20... | collective-permute-start | bytes 98312 | tf_op jit(solution)/shard_map/ppermute | solution.py:26
  83.3 8.3 %collective-permute-start.29 = (bf16[2,32,256]{2,1,0:T(8,128)(2,1)S(1)}, bf16[2,32,256]{2,1,0:T(8,128)(2,1)S(1)}, u32[]{:S(2)}, u32[]{:S(2)}) collective-permute-start(bf16[2,32,256]{2,1,0:T(8,128)(2,1)S(1)} %convolution_convert_fusion.2), channel_id=1, source_target_pairs={{0,2},{2,4},{4,6},{6,8},{8,10},{10,12},{12,14},{14,16},{16,18},{18... | collective-permute-start | bytes 98312 | tf_op jit(solution)/shard_map/ppermute | solution.py:26
  94.4 8.3 %collective-permute-start.31 = (bf16[2,32,256]{2,1,0:T(8,128)(2,1)S(1)}, bf16[2,32,256]{2,1,0:T(8,128)(2,1)S(1)}, u32[]{:S(2)}, u32[]{:S(2)}) collective-permute-start(bf16[2,32,256]{2,1,0:T(8,128)(2,1)S(1)} %convolution_convert_fusion.1), channel_id=1, source_target_pairs={{0,2},{2,4},{4,6},{6,8},{8,10},{10,12},{12,14},{14,16},{16,18},{18... | collective-permute-start | bytes 98312 | tf_op jit(solution)/shard_map/ppermute | solution.py:26
  (16 other events, 240.8 us)
